TPU v7x, 256 devices: a whole 4x4x8 slice. The times are simulated.
256 devices in a mesh: dp: 4 (over y), expert: 64 (over z, x, core).
Axes of the slice: x: 4, y: 4, z: 8, core: 2. Of those that a mesh axis runs over, the one named last changes fastest.
Arguments:
- tokens: bfloat16 [32768, 2048], P(('dp', 'expert')), may hold values from -6 to 6
- cotangent: bfloat16 [32768, 2048], P(('dp', 'expert')), may hold values from -3 to 3
- routes: int32 [32768, 1], P(('dp', 'expert')), may hold values from 0 to 63, as said below
- gate_fixed: int32 [32768, 1], P(('dp', 'expert')), may hold values from 8192 to 65535
- w_gate: bfloat16 [64, 2048, 768], P('expert', 'dp'), may hold values from -0.125 to 0.125
- w_up: bfloat16 [64, 2048, 768], P('expert', 'dp'), may hold values from -0.125 to 0.125
- w_down: bfloat16 [64, 768, 2048], P('expert', None, 'dp'), may hold values from -0.21875 to 0.21875
Outputs:
- mixed: bfloat16 [32768, 2048], P(('dp', 'expert'))
- grad_tokens: bfloat16 [32768, 2048], P(('dp', 'expert'))
- grad_w_gate: bfloat16 [64, 2048, 768], P('expert', 'dp')
- grad_w_up: bfloat16 [64, 2048, 768], P('expert', 'dp')
- grad_w_down: bfloat16 [64, 768, 2048], P('expert', None, 'dp')
Inputs may be any that keep to these rules, and one draw needn't show every extreme that they name: `routes`: each token names one expert. Among the tokens of one device no expert is named more than 3 times, and some experts are named exactly 3 times by the tokens of every device.
All inputs are finite; a program needn't handle non-finite values.
Results may differ from a plain program's by a relative error of at most 0.0058.
Values may be sent and summed in bfloat16 or wider, within the bound.
A program may use at most 64 MiB of HBM per device.

v0:
```python
import jax
import jax.numpy as jnp
from jax import lax
from jax.sharding import Mesh
from jax.sharding import PartitionSpec as P

EXPERT = ("expert_0", "expert_1", "expert_2")
DP_EXPERT = ("dp", "expert_0", "expert_1", "expert_2")


def in_blocks(array, dim, size):
    lengths = array.shape
    tiles = array.reshape(*lengths[:dim], size, lengths[dim] // size, *lengths[dim + 1 :])
    return jnp.moveaxis(tiles, dim, 0)


def joined_along(tiles, dim):
    tiles = jnp.moveaxis(tiles, 0, dim)
    lengths = tiles.shape
    return tiles.reshape(*lengths[:dim], lengths[dim] * lengths[dim + 1], *lengths[dim + 2 :])


def turned_blocks(tiles, axes, turns):
    lengths = [lax.axis_size(a) for a in axes]
    tiles = tiles.reshape(*lengths, *tiles.shape[1:])
    for k in turns:
        tiles = lax.all_to_all(tiles, axes[k], split_axis=k, concat_axis=k, tiled=True)
    return tiles.reshape(-1, *tiles.shape[len(axes) :])


def two_step_exchange(array, groups, turns, split_dim, concat_dim):
    size = lax.axis_size(groups[0]) * lax.axis_size(groups[1])
    tiles = in_blocks(array, split_dim, size)
    return joined_along(turned_blocks(tiles, groups, turns), concat_dim)


def gather_turned(arrays, axis, dims):
    turned = [jnp.moveaxis(a, dim, 0) for a, dim in zip(arrays, dims)]
    widths = [t[0].size for t in turned]
    both = jnp.concatenate([t.reshape(-1, w) for t, w in zip(turned, widths)], axis=1)
    filled = lax.all_gather(both, axis, axis=0, tiled=True)
    tiles = jnp.split(filled, [sum(widths[:k]) for k in range(1, len(widths))], axis=1)
    return tuple(
        (
            jnp.moveaxis(b.reshape(-1, *t.shape[1:]), 0, dim)
            for b, t, dim in zip(tiles, turned, dims)
        )
    )


def sent_together(arrays, axis, split_dim, concat_dim, along):
    ends, at = ([], 0)
    for a in arrays[:-1]:
        at += a.shape[along]
        ends.append(at)
    both = jnp.concatenate(arrays, axis=along)
    return tuple(
        jnp.split(
            lax.all_to_all(both, axis, split_axis=split_dim, concat_axis=concat_dim, tiled=True),
            ends,
            axis=along,
        )
    )


def in_one_piece(arrays, axis, dim, along):
    both = jnp.concatenate(arrays, axis=along)
    filled, at, gathered = (lax.all_gather(both, axis, axis=dim, tiled=True), 0, [])
    for a in arrays:
        gathered.append(lax.slice_in_dim(filled, at, at + a.shape[along], axis=along))
        at += a.shape[along]
    return tuple(gathered)


def swap_experts(buffer):
    return two_step_exchange(buffer, (("expert_0", "expert_1"), "expert_2"), (0, 1), 1, 1)


def contract_last(left_side, right_side):
    return lax.dot_general(
        left_side, right_side, (((1,), (1,)), ((), ())), preferred_element_type=jnp.float32
    )


def contract_first(left_side, right_side):
    return lax.dot_general(
        left_side, right_side, (((0,), (0,)), ((), ())), preferred_element_type=jnp.float32
    )


def gate_gradients(grad_hidden, gate_pre, up_pre):
    sigmoid_gate = jax.nn.sigmoid(gate_pre)
    grad_gate = grad_hidden * up_pre * sigmoid_gate * (1.0 + gate_pre * (1.0 - sigmoid_gate))
    grad_up = grad_hidden * gate_pre * sigmoid_gate
    return jnp.concatenate([grad_gate, grad_up], axis=1).astype(jnp.bfloat16)


def full_width_pass(outgoing, grad_outgoing, gate_up_w, down_all, shape_out):
    expert_count, capacity, model_width = shape_out
    own_rows = expert_count * capacity
    hidden_width = down_all.shape[0]
    received = swap_experts(outgoing)
    flat_received = received.reshape(own_rows, model_width)
    gate_up = jnp.dot(flat_received, gate_up_w, preferred_element_type=jnp.float32)
    gate_pre = gate_up[:, :hidden_width]
    up_pre = gate_up[:, hidden_width:]
    hidden = (gate_pre * jax.nn.sigmoid(gate_pre) * up_pre).astype(jnp.bfloat16)
    slot_out = jnp.dot(hidden, down_all, preferred_element_type=jnp.float32).astype(jnp.bfloat16)
    returned = swap_experts(slot_out.reshape(1, expert_count, capacity, model_width)).reshape(
        own_rows, model_width
    )
    grad_received = swap_experts(grad_outgoing)
    grad_hidden = contract_last(grad_received.reshape(own_rows, model_width), down_all)
    grad_gate_up = gate_gradients(grad_hidden, gate_pre, up_pre)
    slot_grad_in = contract_last(grad_gate_up, gate_up_w).astype(jnp.bfloat16)
    grad_returned = swap_experts(
        slot_grad_in.reshape(1, expert_count, capacity, model_width)
    ).reshape(own_rows, model_width)
    return (received, grad_received, hidden, grad_gate_up, returned, grad_returned)


def body(tokens, cotangent, routes, gate_fixed, w_gate, w_up, w_down):
    tok_count = tokens.shape[0]
    model_width = tokens.shape[1]
    route_count = routes.shape[1]
    hidden_width = w_gate.shape[2]
    expert_count = lax.axis_size(EXPERT)
    capacity = 3 * tok_count * route_count // (2 * expert_count)
    own_rows = expert_count * capacity
    flat_total = tok_count * route_count
    route_weight = gate_fixed.astype(jnp.float32) / 65536.0
    flat_routes = routes.reshape(flat_total)
    one_hot = (flat_routes[:, None] == jnp.arange(expert_count, dtype=jnp.int32)[None, :]).astype(
        jnp.int32
    )
    position = jnp.sum((jnp.cumsum(one_hot, axis=0) - one_hot) * one_hot, axis=1)
    slot_index = flat_routes * capacity + position
    matches = slot_index[None, :] == jnp.arange(own_rows, dtype=jnp.int32)[:, None]
    occupied = jnp.any(matches, axis=1)
    source_row = jnp.sum(
        jnp.where(matches, jnp.arange(flat_total, dtype=jnp.int32)[None, :], 0), axis=1
    )
    slot_weight = jnp.sum(
        jnp.where(matches, route_weight.reshape(flat_total)[None, :], 0.0), axis=1
    )
    token_row = source_row // route_count
    outgoing = jnp.where(
        occupied[:, None], jnp.take(tokens, token_row, axis=0), jnp.zeros((), tokens.dtype)
    )
    outgoing = outgoing.reshape(1, expert_count, capacity, model_width)
    scaled = (
        slot_weight[:, None] * jnp.take(cotangent, token_row, axis=0).astype(jnp.float32)
    ).astype(jnp.bfloat16)
    grad_outgoing = jnp.where(occupied[:, None], scaled, jnp.zeros((), scaled.dtype))
    grad_outgoing = grad_outgoing.reshape(1, expert_count, capacity, model_width)
    shape_out = (expert_count, capacity, model_width)
    replicas = lax.axis_size("dp")
    part_width = model_width // replicas
    gate_all, up_all, down_all = gather_turned((w_gate[0], w_up[0], w_down[0]), "dp", (0, 0, 1))
    gate_up_w = jnp.concatenate([gate_all, up_all], axis=1)
    received, grad_received, hidden, grad_gate_up, returned, grad_returned = full_width_pass(
        outgoing, grad_outgoing, gate_up_w, down_all, shape_out
    )
    slot_cols, grad_cols = sent_together((received, grad_received), "dp", 3, 0, 1)
    hidden_all, grad_gate_up_all = in_one_piece((hidden, grad_gate_up), "dp", 0, 1)
    slot_cols = slot_cols.reshape(replicas * own_rows, part_width)
    grad_cols = grad_cols.reshape(replicas * own_rows, part_width)
    gate_up_grad = contract_first(slot_cols, grad_gate_up_all)
    down_grad = contract_first(hidden_all, grad_cols)
    picked = (
        jnp.take(returned, slot_index, axis=0)
        .reshape(tok_count, route_count, model_width)
        .astype(jnp.float32)
    )
    mixed = jnp.sum(route_weight[:, :, None] * picked, axis=1).astype(jnp.bfloat16)
    grad_picked = (
        jnp.take(grad_returned, slot_index, axis=0)
        .reshape(tok_count, route_count, model_width)
        .astype(jnp.float32)
    )
    grad_tokens = jnp.sum(grad_picked, axis=1).astype(jnp.bfloat16)
    grad_w_gate = gate_up_grad[:, :hidden_width].astype(jnp.bfloat16)[None]
    grad_w_up = gate_up_grad[:, hidden_width:].astype(jnp.bfloat16)[None]
    grad_w_down = down_grad.astype(jnp.bfloat16)[None]
    return (mixed, grad_tokens, grad_w_gate, grad_w_up, grad_w_down)


def solution(mesh):
    finer = Mesh(
        mesh.devices.reshape(mesh.shape["dp"], 8, 4, 2), ("dp", "expert_0", "expert_1", "expert_2")
    )
    placed = (
        P(DP_EXPERT, None),
        P(DP_EXPERT, None),
        P(DP_EXPERT, None),
        P(DP_EXPERT, None),
        P(EXPERT, "dp", None),
        P(EXPERT, "dp", None),
        P(EXPERT, None, "dp"),
    )
    return jax.shard_map(
        body,
        mesh=finer,
        in_specs=placed,
        out_specs=(
            P(DP_EXPERT, None),
            P(DP_EXPERT, None),
            P(EXPERT, "dp", None),
            P(EXPERT, "dp", None),
            P(EXPERT, None, "dp"),
        ),
        check_vma=False,
    )
```

profile of v0, /device:TPU:1, one launch (start us, length us, event | category | flops | bytes accessed | tf_op | source)
XLA Modules:
  0.0 254.6 jit_solution(7288200320655958101)
XLA Ops:
  21.4 11.9 %all-to-all-start = ((bf16[32,2,1,1,3,2048]{5,1,4,3,2,0:T(2,128)(2,1)}), bf16[32,2,1,1,3,2048]{5,1,4,3,2,0:T(2,128)(2,1)S(1)}, u32[]{:S(2)}, u32[]{:S(2)}) async-start(bf16[32,2,1,1,3,2048]{5,1,4,3,2,0:T(2,128)(2,1)} %copy.57), calls=%async_computation | async-start | bytes 1572864 | tf_op jit(solution)/shard_map/all_to_all | solution.py:27
  35.7 18.7 %all-to-all-done = bf16[32,2,1,1,3,2048]{5,1,4,3,2,0:T(2,128)(2,1)S(1)} async-done(((bf16[32,2,1,1,3,2048]{5,1,4,3,2,0:T(2,128)(2,1)}), bf16[32,2,1,1,3,2048]{5,1,4,3,2,0:T(2,128)(2,1)S(1)}, u32[]{:S(2)}, u32[]{:S(2)}) %all-to-all-start) | async-done | bytes 786464 | tf_op jit(solution)/shard_map/all_to_all | solution.py:27
  54.6 6.8 %all_to_all.58 = bf16[32,2,1,1,3,2048]{5,0,4,3,2,1:T(8,128)(2,1)S(1)} all-to-all(bf16[32,2,1,1,3,2048]{5,0,4,3,2,1:T(8,128)(2,1)S(1)} %copy.58), channel_id=1, replica_groups=mesh['dp'=4,'expert_0'=8,'expert_1'=4,'expert_2'=2] {'expert_2'}, dimensions={1} | all-to-all | bytes 1572864 | tf_op jit(solution)/shard_map/all_to_all | solution.py:27
  61.4 4.8 %all-to-all-start.4 = ((bf16[32,2,1,1,3,2048]{5,1,4,3,2,0:T(2,128)(2,1)}), bf16[32,2,1,1,3,2048]{5,1,4,3,2,0:T(2,128)(2,1)S(1)}, u32[]{:S(2)}, u32[]{:S(2)}) async-start(bf16[32,2,1,1,3,2048]{5,1,4,3,2,0:T(2,128)(2,1)} %copy.65), calls=%async_computation.4 | async-start | bytes 1572864 | tf_op jit(solution)/shard_map/all_to_all | solution.py:27
  68.4 19.1 %all-to-all-done.4 = bf16[32,2,1,1,3,2048]{5,1,4,3,2,0:T(2,128)(2,1)S(1)} async-done(((bf16[32,2,1,1,3,2048]{5,1,4,3,2,0:T(2,128)(2,1)}), bf16[32,2,1,1,3,2048]{5,1,4,3,2,0:T(2,128)(2,1)S(1)}, u32[]{:S(2)}, u32[]{:S(2)}) %all-to-all-start.4) | async-done | bytes 786464 | tf_op jit(solution)/shard_map/all_to_all | solution.py:27
  87.8 6.8 %all_to_all.59 = bf16[32,2,1,1,3,2048]{5,0,4,3,2,1:T(8,128)(2,1)S(1)} all-to-all(bf16[32,2,1,1,3,2048]{5,0,4,3,2,1:T(8,128)(2,1)S(1)} %copy.66), channel_id=1, replica_groups=mesh['dp'=4,'expert_0'=8,'expert_1'=4,'expert_2'=2] {'expert_2'}, dimensions={1} | all-to-all | bytes 1572864 | tf_op jit(solution)/shard_map/all_to_all | solution.py:27
  96.7 13.3 %all-gather.3.cloned.1.call-done = bf16[2048,2304]{0,1:T(8,128)(2,1)} async-done(((bf16[512,2304]{0,1:T(8,128)(2,1)}), bf16[2048,2304]{0,1:T(8,128)(2,1)}) %all-gather.3.cloned.1.call-update) | async-done | bytes 9437200 | tf_op jit(solution)/shard_map/all_gather | solution.py:41
  110.0 5.3 %fusion.2 = f32[192,1536]{1,0:T(8,128)S(1)} fusion(bf16[192,2048]{1,0:T(8,128)(2,1)} %reshape_reshape_transpose_reshape.12, bf16[2048,2304]{0,1:T(8,128)(2,1)} %all-gather.3.cloned.1.call-done), kind=kOutput, calls=%fused_computation.6 | convolution fusion | flops 1207959552 | bytes 8257536 | tf_op jit(solution)/shard_map/dot_general | solution.py:104
  115.3 3.3 %multiply_convert_fusion.3 = (bf16[192,768]{1,0:T(8,128)(2,1)S(1)}, bf16[192,768]{1,0:T(8,128)(2,1)S(1)}, bf16[192,768]{1,0:T(8,128)(2,1)S(1)}) fusion(f32[192,1536]{1,0:T(8,128)S(1)} %fusion.2, bf16[192,2048]{1,0:T(8,128)(2,1)S(1)} %copy-done.6, bf16[2048,2304]{0,1:T(8,128)(2,1)} %all-gather.3.cloned.1.call-done), kind=kOutput, calls=%fused_computation.32 | convolution fusion | flops 606339072 | bytes 5996544 | tf_op jit(solution)/shard_map/dot_general | solution.py:80
  120.3 3.6 %fusion.8 = bf16[192,2048]{1,0:T(8,128)(2,1)} fusion(bf16[192,768]{1,0:T(8,128)(2,1)S(1)} %get-tuple-element.15, bf16[2048,2304]{0,1:T(8,128)(2,1)} %all-gather.3.cloned.1.call-done), kind=kOutput, calls=%fused_computation.13 | convolution fusion | flops 604372992 | bytes 4227072 | tf_op jit(solution)/shard_map/dot_general | solution.py:108
  128.2 9.5 %all-to-all-start.2 = ((bf16[32,2,1,1,3,2048]{5,1,4,3,2,0:T(2,128)(2,1)}), bf16[32,2,1,1,3,2048]{5,1,4,3,2,0:T(2,128)(2,1)S(1)}, u32[]{:S(2)}, u32[]{:S(2)}) async-start(bf16[32,2,1,1,3,2048]{5,1,4,3,2,0:T(2,128)(2,1)} %copy.62), calls=%async_computation.2 | async-start | bytes 1572864 | tf_op jit(solution)/shard_map/all_to_all | solution.py:27
  139.4 3.0 %reshape_transpose_reshape.7 = bf16[1,64,3,2048]{3,1,2,0:T(8,128)(2,1)} reshape(bf16[32,2,1,1,3,2048]{5,1,0,4,3,2:T(2,128)(2,1)} %copy.72) | data formatting | bytes 1572864 | tf_op jit(solution)/shard_map/reshape;transpose;reshape | solution.py:20
  148.4 10.4 %all-to-all-done.2 = bf16[32,2,1,1,3,2048]{5,1,4,3,2,0:T(2,128)(2,1)S(1)} async-done(((bf16[32,2,1,1,3,2048]{5,1,4,3,2,0:T(2,128)(2,1)}), bf16[32,2,1,1,3,2048]{5,1,4,3,2,0:T(2,128)(2,1)S(1)}, u32[]{:S(2)}, u32[]{:S(2)}) %all-to-all-start.2) | async-done | bytes 786464 | tf_op jit(solution)/shard_map/all_to_all | solution.py:27
  158.7 3.8 %all-to-all-start.8 = ((bf16[1,128,3,2048]{1,2,0,3:T(4,128)(2,1)}), bf16[1,128,3,2048]{1,2,0,3:T(4,128)(2,1)S(1)}, u32[]{:S(2)}, u32[]{:S(2)}) async-start(bf16[1,128,3,2048]{1,2,0,3:T(4,128)(2,1)} %copy.73), calls=%async_computation.8 | async-start | bytes 4194304 | tf_op jit(solution)/shard_map/all_to_all | solution.py:59
  162.6 5.2 %fusion.11 = bf16[192,2048]{1,0:T(8,128)(2,1)} fusion(bf16[2048,2304]{0,1:T(8,128)(2,1)} %all-gather.3.cloned.1.call-done, bf16[192,768]{1,0:T(8,128)(2,1)} %copy-done.7, bf16[192,768]{1,0:T(8,128)(2,1)S(1)} %get-tuple-element.9), kind=kOutput, calls=%fused_computation.14 | convolution fusion | flops 1209532416 | bytes 7667712 | tf_op jit(solution)/shard_map/dot_general | solution.py:80
  167.8 3.3 %reshape_transpose_reshape_reshape.15 = bf16[32,2,1,1,3,2048]{5,4,1,0,3,2:T(4,128)(2,1)} reshape(bf16[192,2048]{1,0:T(8,128)(2,1)} %fusion.11) | data formatting | bytes 1572864 | tf_op jit(solution)/shard_map/reshape;transpose;reshape;reshape | solution.py:25
  171.0 3.1 %copy.68 = bf16[32,2,1,1,3,2048]{5,1,4,3,2,0:T(2,128)(2,1)} copy(bf16[32,2,1,1,3,2048]{5,4,1,0,3,2:T(4,128)(2,1)} %reshape_transpose_reshape_reshape.15) | data formatting | bytes 1572864 | tf_op jit(solution)/shard_map/reshape;transpose;reshape;reshape | solution.py:25
  175.3 10.9 %all-to-all-done.8 = bf16[1,128,3,2048]{1,2,0,3:T(4,128)(2,1)S(1)} async-done(((bf16[1,128,3,2048]{1,2,0,3:T(4,128)(2,1)}), bf16[1,128,3,2048]{1,2,0,3:T(4,128)(2,1)S(1)}, u32[]{:S(2)}, u32[]{:S(2)}) %all-to-all-start.8) | async-done | bytes 1572896 | tf_op jit(solution)/shard_map/all_to_all | solution.py:59
  186.1 9.8 %all_to_all.60 = bf16[32,2,1,1,3,2048]{5,0,4,3,2,1:T(8,128)(2,1)} all-to-all(bf16[32,2,1,1,3,2048]{5,0,4,3,2,1:T(8,128)(2,1)} %copy.63), channel_id=1, replica_groups=mesh['dp'=4,'expert_0'=8,'expert_1'=4,'expert_2'=2] {'expert_2'}, dimensions={1} | all-to-all | bytes 1572864 | tf_op jit(solution)/shard_map/all_to_all | solution.py:27
  196.0 9.6 %all-to-all-start.6 = ((bf16[32,2,1,1,3,2048]{5,1,4,3,2,0:T(2,128)(2,1)}), bf16[32,2,1,1,3,2048]{5,1,4,3,2,0:T(2,128)(2,1)}, u32[]{:S(2)}, u32[]{:S(2)}) async-start(bf16[32,2,1,1,3,2048]{5,1,4,3,2,0:T(2,128)(2,1)} %copy.68), calls=%async_computation.6 | async-start | bytes 1572864 | tf_op jit(solution)/shard_map/all_to_all | solution.py:27
  217.1 9.8 %all-to-all-done.6 = bf16[32,2,1,1,3,2048]{5,1,4,3,2,0:T(2,128)(2,1)} async-done(((bf16[32,2,1,1,3,2048]{5,1,4,3,2,0:T(2,128)(2,1)}), bf16[32,2,1,1,3,2048]{5,1,4,3,2,0:T(2,128)(2,1)}, u32[]{:S(2)}, u32[]{:S(2)}) %all-to-all-start.6) | async-done | bytes 786464 | tf_op jit(solution)/shard_map/all_to_all | solution.py:27
  228.3 6.7 %all_to_all.61 = bf16[32,2,1,1,3,2048]{5,0,4,3,2,1:T(8,128)(2,1)S(1)} all-to-all(bf16[32,2,1,1,3,2048]{5,0,4,3,2,1:T(8,128)(2,1)S(1)} %copy.69), channel_id=1, replica_groups=mesh['dp'=4,'expert_0'=8,'expert_1'=4,'expert_2'=2] {'expert_2'}, dimensions={1} | all-to-all | bytes 1572864 | tf_op jit(solution)/shard_map/all_to_all | solution.py:27
  240.3 3.1 %convolution_convert_fusion = bf16[512,1536]{1,0:T(8,128)(2,1)S(1)} fusion(bf16[768,512]{1,0:T(8,128)(2,1)S(1)} %copy-done.5, bf16[768,2304]{1,0:T(8,128)(2,1)} %all-gather.5.cloned.1.call-done), kind=kOutput, calls=%fused_computation.8 | convolution fusion | flops 1208745984 | bytes 4718592 | tf_op jit(solution)/shard_map/dot_general | solution.py:86
  244.8 3.0 %fusion.15 = bf16[1,768,512]{2,1,0:T(8,128)(2,1)} fusion(bf16[768,512]{1,0:T(8,128)(2,1)S(1)} %copy-done.4, bf16[768,2304]{1,0:T(8,128)(2,1)} %all-gather.5.cloned.1.call-done), kind=kOutput, calls=%fused_computation.20 | convolution fusion | flops 604372992 | bytes 2752512 | tf_op jit(solution)/shard_map/dot_general | solution.py:86
  (79 shorter events, 55.6 us)
Async XLA Ops:
  7.2 5.8 %copy-start = (bf16[128,2048]{1,0:T(8,128)(2,1)S(1)}, bf16[128,2048]{1,0:T(8,128)(2,1)}, u32[]{:S(2)}) copy-start(bf16[128,2048]{1,0:T(8,128)(2,1)} %param.12) | copy-start | bytes 1572868
  7.2 3.0 %copy-start.3 = (bf16[1,768,512]{2,1,0:T(8,128)(2,1)S(1)}, bf16[1,768,512]{2,1,0:T(8,128)(2,1)}, u32[]{:S(2)}) copy-start(bf16[1,768,512]{2,1,0:T(8,128)(2,1)} %param.17) | copy-start | bytes 2359300
  7.2 102.8 %all-gather.3.cloned.1.call-start = ((), (), s32[]{:S(2)}) async-start(), calls=%async_computation.9 | async-start | bytes 11796480 | tf_op jit(solution)/shard_map/all_gather | solution.py:41
  11.7 0.7 copy-start.8
  13.0 2.0 copy-start.2
  15.0 2.1 copy-start.9
  21.4 32.9 %all-to-all-start = ((bf16[32,2,1,1,3,2048]{5,1,4,3,2,0:T(2,128)(2,1)}), bf16[32,2,1,1,3,2048]{5,1,4,3,2,0:T(2,128)(2,1)S(1)}, u32[]{:S(2)}, u32[]{:S(2)}) async-start(bf16[32,2,1,1,3,2048]{5,1,4,3,2,0:T(2,128)(2,1)} %copy.57), calls=%async_computation | async-start | bytes 1572864 | tf_op jit(solution)/shard_map/all_to_all | solution.py:27
  61.4 26.2 %all-to-all-start.4 = ((bf16[32,2,1,1,3,2048]{5,1,4,3,2,0:T(2,128)(2,1)}), bf16[32,2,1,1,3,2048]{5,1,4,3,2,0:T(2,128)(2,1)S(1)}, u32[]{:S(2)}, u32[]{:S(2)}) async-start(bf16[32,2,1,1,3,2048]{5,1,4,3,2,0:T(2,128)(2,1)} %copy.65), calls=%async_computation.4 | async-start | bytes 1572864 | tf_op jit(solution)/shard_map/all_to_all | solution.py:27
  66.2 174.1 %all-gather.5.cloned.1.call-start = ((), (), s32[]{:S(2)}) async-start(), calls=%async_computation.10 | async-start | bytes 4423680 | tf_op jit(solution)/shard_map/all_gather | solution.py:68
  96.7 18.6 %copy-start.6 = (bf16[192,2048]{1,0:T(8,128)(2,1)S(1)}, bf16[192,2048]{1,0:T(8,128)(2,1)}, u32[]{:S(2)}) copy-start(bf16[192,2048]{1,0:T(8,128)(2,1)} %reshape_reshape_transpose_reshape.14) | copy-start | bytes 2359300
  118.5 0.7 copy-start.7
  128.2 30.6 %all-to-all-start.2 = ((bf16[32,2,1,1,3,2048]{5,1,4,3,2,0:T(2,128)(2,1)}), bf16[32,2,1,1,3,2048]{5,1,4,3,2,0:T(2,128)(2,1)S(1)}, u32[]{:S(2)}, u32[]{:S(2)}) async-start(bf16[32,2,1,1,3,2048]{5,1,4,3,2,0:T(2,128)(2,1)} %copy.62), calls=%async_computation.2 | async-start | bytes 1572864 | tf_op jit(solution)/shard_map/all_to_all | solution.py:27
  158.7 27.4 %all-to-all-start.8 = ((bf16[1,128,3,2048]{1,2,0,3:T(4,128)(2,1)}), bf16[1,128,3,2048]{1,2,0,3:T(4,128)(2,1)S(1)}, u32[]{:S(2)}, u32[]{:S(2)}) async-start(bf16[1,128,3,2048]{1,2,0,3:T(4,128)(2,1)} %copy.73), calls=%async_computation.8 | async-start | bytes 4194304 | tf_op jit(solution)/shard_map/all_to_all | solution.py:59
  196.0 30.9 %all-to-all-start.6 = ((bf16[32,2,1,1,3,2048]{5,1,4,3,2,0:T(2,128)(2,1)}), bf16[32,2,1,1,3,2048]{5,1,4,3,2,0:T(2,128)(2,1)}, u32[]{:S(2)}, u32[]{:S(2)}) async-start(bf16[32,2,1,1,3,2048]{5,1,4,3,2,0:T(2,128)(2,1)} %copy.68), calls=%async_computation.6 | async-start | bytes 1572864 | tf_op jit(solution)/shard_map/all_to_all | solution.py:27
  237.4 3.0 %copy-start.5 = (bf16[768,512]{1,0:T(8,128)(2,1)S(1)}, bf16[768,512]{1,0:T(8,128)(2,1)}, u32[]{:S(2)}) copy-start(bf16[768,512]{1,0:T(8,128)(2,1)} %reshape.53) | copy-start | bytes 2359300
  243.4 1.4 copy-start.4
  243.4 4.3 %copy-start.1 = (bf16[128,2048]{1,0:T(8,128)(2,1)S(1)}, bf16[128,2048]{1,0:T(8,128)(2,1)}, u32[]{:S(2)}) copy-start(bf16[128,2048]{1,0:T(8,128)(2,1)} %param.12) | copy-start | bytes 1572868
Sparse Core Ops, SparseCore 0:
  11.9 98.0 all-gather.2
  120.4 46.3 all-gather.4
where the time goes:
time: 256 us; the launch traced here: 255 us
  waiting for transfers between devices  82.2 us (32%)
  local copies, waits for them, and re-layouts  56.2 us (22%)
  starting transfers between devices  39.8 us (16%)
  blocking collectives  30.1 us (12%)
  matrix products  23.3 us (9%)
  between operations  14.4 us (6%)
  other arithmetic  8.59 us (3%)
    all_to_all x4, waiting for transfers between devices, turned_blocks(): lax.all_to_all(tiles, axes[k], split_axis=k, concat_axis=k, tiled=True)  58 us
    all_to_all x4, starting transfers between devices, turned_blocks(): lax.all_to_all(tiles, axes[k], split_axis=k, concat_axis=k, tiled=True)  35.9 us
    all_to_all x4, blocking collectives, turned_blocks(): lax.all_to_all(tiles, axes[k], split_axis=k, concat_axis=k, tiled=True)  30.1 us
    another operation x8, local copies, waits for them, and re-layouts, turned_blocks(): tiles = tiles.reshape(*lengths, *tiles.shape[1:])  15.4 us
    all_gather x1, waiting for transfers between devices, gather_turned(): filled = lax.all_gather(both, axis, axis=0, tiled=True)  13.3 us
    all_to_all x1, waiting for transfers between devices, sent_together(): lax.all_to_all(both, axis, split_axis=split_dim, concat_axis=concat_dim,...  10.9 us
    all_to_all x10, local copies, waits for them, and re-layouts, turned_blocks(): lax.all_to_all(tiles, axes[k], split_axis=k, concat_axis=k, tiled=True)  9.33 us
    dot_general x2, matrix products, contract_last(): lax.dot_general(left_side, right_side, (((1,), (1,)), ((), ())), preferre...  8.43 us
  transfers between devices with their start and end apart: 7, of which 6 were waited for; matrix products, arithmetic and copies ran while one was open for 26% of the time, Pallas kernels for 0%

commit v1 on v0

--- a/solution.py
+++ b/solution.py
@@ -38,7 +38,9 @@
     turned = [jnp.moveaxis(a, dim, 0) for a, dim in zip(arrays, dims)]
     widths = [t[0].size for t in turned]
     both = jnp.concatenate([t.reshape(-1, w) for t, w in zip(turned, widths)], axis=1)
-    filled = lax.all_gather(both, axis, axis=0, tiled=True)
+    filled = jnp.concatenate(
+        jax.lax.all_to_all(jnp.stack([both] * jax.lax.axis_size(axis), axis=0), axis, 0, 0), axis=0
+    )
     tiles = jnp.split(filled, [sum(widths[:k]) for k in range(1, len(widths))], axis=1)
     return tuple(
         (

time: 256 us -> 347 us (1.36)
  waiting for transfers between devices: 82.2 us -> 163 us
  starting transfers between devices: 39.8 us -> 50.2 us
  blocking collectives: 30.1 us -> 22.4 us
  local copies, waits for them, and re-layouts: 56.2 us -> 62 us
    all_to_all x0 -> x1, waiting for transfers between devices: none -> 99.9 us  [gather_turned(): jax.lax.all_to_all(jnp.stack([both] * jax.lax.axis_size(axis), axis=0), a...]
    all_gather x1 -> x0, waiting for transfers between devices: 13.3 us -> none  [gather_turned(): filled = lax.all_gather(both, axis, axis=0, tiled=True)]
    all_to_all x4 -> x3, blocking collectives: 30.1 us -> 22.4 us  [turned_blocks(): lax.all_to_all(tiles, axes[k], split_axis=k, concat_axis=k, tiled=True)]
    all_to_all x4 -> x5, waiting for transfers between devices: 58 us -> 51.1 us  [turned_blocks(): lax.all_to_all(tiles, axes[k], split_axis=k, concat_axis=k, tiled=True)]
    all_to_all x0 -> x1, starting transfers between devices: none -> 5.82 us  [gather_turned(): jax.lax.all_to_all(jnp.stack([both] * jax.lax.axis_size(axis), axis=0), a...]
    all_to_all x10, local copies, waits for them, and re-layouts: 9.33 us -> 14.8 us  [turned_blocks(): lax.all_to_all(tiles, axes[k], split_axis=k, concat_axis=k, tiled=True)]
    all_to_all x4 -> x5, starting transfers between devices: 35.9 us -> 40.4 us  [turned_blocks(): lax.all_to_all(tiles, axes[k], split_axis=k, concat_axis=k, tiled=True)]
    another operation x0 -> x1, local copies, waits for them, and re-layouts: none -> 4.26 us  [gather_turned(): jnp.stack([both] * jax.lax.axis_size(axis), axis=0)]
  transfers between devices with their start and end apart: 7 -> 8, of which waited for: 6 -> 6; matrix products, arithmetic and copies ran while one was open for 26% -> 19% of each run, Pallas kernels for 0% -> 0%
where the time goes in v1:
time: 347 us; the launch traced here: 345 us
  waiting for transfers between devices  163 us (47%)
  local copies, waits for them, and re-layouts  62 us (18%)
  starting transfers between devices  50.2 us (14%)
  blocking collectives  22.4 us (6%)
  matrix products  22.3 us (6%)
  between operations  14.4 us (4%)
  other arithmetic  10.8 us (3%)
    all_to_all x1, waiting for transfers between devices, gather_turned(): jax.lax.all_to_all(jnp.stack([both] * jax.lax.axis_size(axis), axis=0), a...  99.9 us
    all_to_all x5, waiting for transfers between devices, turned_blocks(): lax.all_to_all(tiles, axes[k], split_axis=k, concat_axis=k, tiled=True)  51.1 us
    all_to_all x5, starting transfers between devices, turned_blocks(): lax.all_to_all(tiles, axes[k], split_axis=k, concat_axis=k, tiled=True)  40.4 us
    all_to_all x3, blocking collectives, turned_blocks(): lax.all_to_all(tiles, axes[k], split_axis=k, concat_axis=k, tiled=True)  22.4 us
    all_to_all x10, local copies, waits for them, and re-layouts, turned_blocks(): lax.all_to_all(tiles, axes[k], split_axis=k, concat_axis=k, tiled=True)  14.8 us
    another operation x8, local copies, waits for them, and re-layouts, turned_blocks(): tiles = tiles.reshape(*lengths, *tiles.shape[1:])  13.5 us
    all_to_all x1, waiting for transfers between devices, sent_together(): lax.all_to_all(both, axis, split_axis=split_dim, concat_axis=concat_dim,...  11.9 us
    dot_general x2, matrix products, contract_last(): lax.dot_general(left_side, right_side, (((1,), (1,)), ((), ())), preferre...  7.89 us
  transfers between devices with their start and end apart: 8, of which 6 were waited for; matrix products, arithmetic and copies ran while one was open for 19% of the time, Pallas kernels for 0%

profile of v1, /device:TPU:1, one launch (start us, length us, event | category | flops | bytes accessed | tf_op | source)
XLA Modules:
  0.0 345.1 jit_solution(15088311088940179623)
XLA Ops:
  18.2 11.9 %all-to-all-start = ((bf16[32,2,1,1,3,2048]{5,1,4,3,2,0:T(2,128)(2,1)}), bf16[32,2,1,1,3,2048]{5,1,4,3,2,0:T(2,128)(2,1)S(1)}, u32[]{:S(2)}, u32[]{:S(2)}) async-start(bf16[32,2,1,1,3,2048]{5,1,4,3,2,0:T(2,128)(2,1)} %copy.61), calls=%async_computation | async-start | bytes 1572864 | tf_op jit(solution)/shard_map/all_to_all | solution.py:27
  32.5 18.7 %all-to-all-done = bf16[32,2,1,1,3,2048]{5,1,4,3,2,0:T(2,128)(2,1)S(1)} async-done(((bf16[32,2,1,1,3,2048]{5,1,4,3,2,0:T(2,128)(2,1)}), bf16[32,2,1,1,3,2048]{5,1,4,3,2,0:T(2,128)(2,1)S(1)}, u32[]{:S(2)}, u32[]{:S(2)}) %all-to-all-start) | async-done | bytes 786464 | tf_op jit(solution)/shard_map/all_to_all | solution.py:27
  51.2 5.9 %all-to-all-start.5 = ((bf16[32,2,1,1,3,2048]{5,1,4,3,2,0:T(2,128)(2,1)}), bf16[32,2,1,1,3,2048]{5,1,4,3,2,0:T(2,128)(2,1)}, u32[]{:S(2)}, u32[]{:S(2)}) async-start(bf16[32,2,1,1,3,2048]{5,1,4,3,2,0:T(2,128)(2,1)} %copy.70), calls=%async_computation.5 | async-start | bytes 1572864 | tf_op jit(solution)/shard_map/all_to_all | solution.py:27
  66.0 10.9 %all-to-all-done.5 = bf16[32,2,1,1,3,2048]{5,1,4,3,2,0:T(2,128)(2,1)} async-done(((bf16[32,2,1,1,3,2048]{5,1,4,3,2,0:T(2,128)(2,1)}), bf16[32,2,1,1,3,2048]{5,1,4,3,2,0:T(2,128)(2,1)}, u32[]{:S(2)}, u32[]{:S(2)}) %all-to-all-start.5) | async-done | bytes 786464 | tf_op jit(solution)/shard_map/all_to_all | solution.py:27
  76.9 8.5 %all-to-all-start.1 = ((bf16[32,2,1,1,3,2048]{5,0,4,3,2,1:T(8,128)(2,1)}), bf16[32,2,1,1,3,2048]{5,0,4,3,2,1:T(8,128)(2,1)}, u32[]{:S(2)}, u32[]{:S(2)}) async-start(bf16[32,2,1,1,3,2048]{5,0,4,3,2,1:T(8,128)(2,1)} %copy.62), calls=%async_computation.1 | async-start | bytes 1572864 | tf_op jit(solution)/shard_map/all_to_all | solution.py:27
  87.6 6.0 %all_to_all.63 = bf16[32,2,1,1,3,2048]{5,0,4,3,2,1:T(8,128)(2,1)} all-to-all(bf16[32,2,1,1,3,2048]{5,0,4,3,2,1:T(8,128)(2,1)} %copy.71), channel_id=1, replica_groups=mesh['dp'=4,'expert_0'=8,'expert_1'=4,'expert_2'=2] {'expert_2'}, dimensions={1} | all-to-all | bytes 1572864 | tf_op jit(solution)/shard_map/all_to_all | solution.py:27
  93.6 4.3 %stack.2 = bf16[4,512,2304]{2,1,0:T(8,128)(2,1)} broadcast(bf16[512,2304]{1,0:T(8,128)(2,1)S(1)} %copy-done.3), dimensions={1,2} | broadcast | bytes 11796480 | tf_op jit(solution)/shard_map/stack | solution.py:42
  97.8 5.8 %all-to-all-start.2 = ((bf16[4,512,2304]{2,1,0:T(8,128)(2,1)}), bf16[4,512,2304]{2,1,0:T(8,128)(2,1)}, u32[]{:S(2)}, u32[]{:S(2)}) async-start(bf16[4,512,2304]{2,1,0:T(8,128)(2,1)} %stack.2), calls=%async_computation.2 | async-start | bytes 18874368 | tf_op jit(solution)/shard_map/all_to_all | solution.py:42
  108.5 99.9 %all-to-all-done.2 = bf16[4,512,2304]{2,1,0:T(8,128)(2,1)} async-done(((bf16[4,512,2304]{2,1,0:T(8,128)(2,1)}), bf16[4,512,2304]{2,1,0:T(8,128)(2,1)}, u32[]{:S(2)}, u32[]{:S(2)}) %all-to-all-start.2) | async-done | bytes 9437216 | tf_op jit(solution)/shard_map/all_to_all | solution.py:42
  208.4 4.5 %fusion.2 = f32[192,1536]{1,0:T(8,128)S(1)} fusion(bf16[192,2048]{1,0:T(8,128)(2,1)} %reshape_reshape_transpose_reshape.12, bf16[2048,2304]{1,0:T(8,128)(2,1)} %bitcast.6), kind=kOutput, calls=%fused_computation.6 | convolution fusion | flops 1207959552 | bytes 8257536 | tf_op jit(solution)/shard_map/dot_general | solution.py:106
  216.7 5.1 %fusion.11 = bf16[192,2048]{1,0:T(8,128)(2,1)S(1)} fusion(bf16[2048,2304]{1,0:T(8,128)(2,1)} %bitcast.6, bf16[192,768]{1,0:T(8,128)(2,1)S(1)} %get-tuple-element.10, bf16[192,768]{1,0:T(8,128)(2,1)S(1)} %get-tuple-element.9), kind=kOutput, calls=%fused_computation.14 | convolution fusion | flops 1209532416 | bytes 7667712 | tf_op jit(solution)/shard_map/dot_general | solution.py:82
  224.2 4.8 %all-to-all-start.7 = ((bf16[32,2,1,1,3,2048]{5,1,4,3,2,0:T(2,128)(2,1)}), bf16[32,2,1,1,3,2048]{5,1,4,3,2,0:T(2,128)(2,1)S(1)}, u32[]{:S(2)}, u32[]{:S(2)}) async-start(bf16[32,2,1,1,3,2048]{5,1,4,3,2,0:T(2,128)(2,1)} %copy.73), calls=%async_computation.7 | async-start | bytes 1572864 | tf_op jit(solution)/shard_map/all_to_all | solution.py:27
  238.2 11.7 %all-to-all-done.7 = bf16[32,2,1,1,3,2048]{5,1,4,3,2,0:T(2,128)(2,1)S(1)} async-done(((bf16[32,2,1,1,3,2048]{5,1,4,3,2,0:T(2,128)(2,1)}), bf16[32,2,1,1,3,2048]{5,1,4,3,2,0:T(2,128)(2,1)S(1)}, u32[]{:S(2)}, u32[]{:S(2)}) %all-to-all-start.7) | async-done | bytes 786464 | tf_op jit(solution)/shard_map/all_to_all | solution.py:27
  249.9 3.8 %all-to-all-start.9 = ((bf16[1,128,3,2048]{1,2,0,3:T(4,128)(2,1)}), bf16[1,128,3,2048]{1,2,0,3:T(4,128)(2,1)S(1)}, u32[]{:S(2)}, u32[]{:S(2)}) async-start(bf16[1,128,3,2048]{1,2,0,3:T(4,128)(2,1)} %copy.78), calls=%async_computation.9 | async-start | bytes 4194304 | tf_op jit(solution)/shard_map/all_to_all | solution.py:61
  253.7 3.9 %fusion.8 = bf16[192,2048]{1,0:T(8,128)(2,1)} fusion(bf16[192,768]{1,0:T(8,128)(2,1)S(1)} %get-tuple-element.15, bf16[2048,2304]{1,0:T(8,128)(2,1)} %bitcast.6), kind=kOutput, calls=%fused_computation.13 | convolution fusion | flops 604372992 | bytes 4227072 | tf_op jit(solution)/shard_map/dot_general | solution.py:110
  257.7 3.3 reshape_transpose_reshape_reshape.13
  260.9 3.1 copy.67
  265.2 11.9 %all-to-all-done.9 = bf16[1,128,3,2048]{1,2,0,3:T(4,128)(2,1)S(1)} async-done(((bf16[1,128,3,2048]{1,2,0,3:T(4,128)(2,1)}), bf16[1,128,3,2048]{1,2,0,3:T(4,128)(2,1)S(1)}, u32[]{:S(2)}, u32[]{:S(2)}) %all-to-all-start.9) | async-done | bytes 1572896 | tf_op jit(solution)/shard_map/all_to_all | solution.py:61
  277.1 9.7 %all_to_all.64 = bf16[32,2,1,1,3,2048]{5,0,4,3,2,1:T(8,128)(2,1)} all-to-all(bf16[32,2,1,1,3,2048]{5,0,4,3,2,1:T(8,128)(2,1)} %copy.74), channel_id=1, replica_groups=mesh['dp'=4,'expert_0'=8,'expert_1'=4,'expert_2'=2] {'expert_2'}, dimensions={1} | all-to-all | bytes 1572864 | tf_op jit(solution)/shard_map/all_to_all | solution.py:27
  286.8 9.4 %all-to-all-start.3 = ((bf16[32,2,1,1,3,2048]{5,1,4,3,2,0:T(2,128)(2,1)}), bf16[32,2,1,1,3,2048]{5,1,4,3,2,0:T(2,128)(2,1)}, u32[]{:S(2)}, u32[]{:S(2)}) async-start(bf16[32,2,1,1,3,2048]{5,1,4,3,2,0:T(2,128)(2,1)} %copy.67), calls=%async_computation.3 | async-start | bytes 1572864 | tf_op jit(solution)/shard_map/all_to_all | solution.py:27
  307.6 9.8 %all-to-all-done.3 = bf16[32,2,1,1,3,2048]{5,1,4,3,2,0:T(2,128)(2,1)} async-done(((bf16[32,2,1,1,3,2048]{5,1,4,3,2,0:T(2,128)(2,1)}), bf16[32,2,1,1,3,2048]{5,1,4,3,2,0:T(2,128)(2,1)}, u32[]{:S(2)}, u32[]{:S(2)}) %all-to-all-start.3) | async-done | bytes 786464 | tf_op jit(solution)/shard_map/all_to_all | solution.py:27
  318.8 6.7 %all_to_all.65 = bf16[32,2,1,1,3,2048]{5,0,4,3,2,1:T(8,128)(2,1)S(1)} all-to-all(bf16[32,2,1,1,3,2048]{5,0,4,3,2,1:T(8,128)(2,1)S(1)} %copy.68), channel_id=1, replica_groups=mesh['dp'=4,'expert_0'=8,'expert_1'=4,'expert_2'=2] {'expert_2'}, dimensions={1} | all-to-all | bytes 1572864 | tf_op jit(solution)/shard_map/all_to_all | solution.py:27
  330.9 3.1 convolution_convert_fusion
  335.3 3.0 fusion.15
  (83 shorter events, 65.3 us)
Async XLA Ops:
  7.2 2.8 copy-start
  9.9 2.0 copy-start.2
  12.0 2.0 copy-start.10
  18.2 32.9 %all-to-all-start = ((bf16[32,2,1,1,3,2048]{5,1,4,3,2,0:T(2,128)(2,1)}), bf16[32,2,1,1,3,2048]{5,1,4,3,2,0:T(2,128)(2,1)S(1)}, u32[]{:S(2)}, u32[]{:S(2)}) async-start(bf16[32,2,1,1,3,2048]{5,1,4,3,2,0:T(2,128)(2,1)} %copy.61), calls=%async_computation | async-start | bytes 1572864 | tf_op jit(solution)/shard_map/all_to_all | solution.py:27
  30.6 26.5 %copy-start.8 = (bf16[1,512,768]{2,1,0:T(8,128)(2,1)S(1)}, bf16[1,512,768]{2,1,0:T(8,128)(2,1)}, u32[]{:S(2)}) copy-start(bf16[1,512,768]{2,1,0:T(8,128)(2,1)} %param.15) | copy-start | bytes 2359300
  32.5 25.8 %copy-start.9 = (bf16[1,512,768]{2,1,0:T(8,128)(2,1)S(1)}, bf16[1,512,768]{2,1,0:T(8,128)(2,1)}, u32[]{:S(2)}) copy-start(bf16[1,512,768]{2,1,0:T(8,128)(2,1)} %param.16) | copy-start | bytes 2359300
  51.2 8.2 %copy-start.5 = (bf16[32,2,1,1,3,2048]{5,1,4,3,2,0:T(2,128)(2,1)}, bf16[32,2,1,1,3,2048]{5,1,4,3,2,0:T(2,128)(2,1)S(1)}, u32[]{:S(2)}) copy-start(bf16[32,2,1,1,3,2048]{5,1,4,3,2,0:T(2,128)(2,1)S(1)} %all-to-all-done) | copy-start | bytes 2359300
  51.2 25.7 %all-to-all-start.5 = ((bf16[32,2,1,1,3,2048]{5,1,4,3,2,0:T(2,128)(2,1)}), bf16[32,2,1,1,3,2048]{5,1,4,3,2,0:T(2,128)(2,1)}, u32[]{:S(2)}, u32[]{:S(2)}) async-start(bf16[32,2,1,1,3,2048]{5,1,4,3,2,0:T(2,128)(2,1)} %copy.70), calls=%async_computation.5 | async-start | bytes 1572864 | tf_op jit(solution)/shard_map/all_to_all | solution.py:27
  66.0 27.6 %copy-start.3 = (bf16[512,2304]{1,0:T(8,128)(2,1)S(1)}, bf16[512,2304]{1,0:T(8,128)(2,1)}, u32[]{:S(2)}) copy-start(bf16[512,2304]{1,0:T(8,128)(2,1)} %copy.66) | copy-start | bytes 7077892
  76.9 10.7 %all-to-all-start.1 = ((bf16[32,2,1,1,3,2048]{5,0,4,3,2,1:T(8,128)(2,1)}), bf16[32,2,1,1,3,2048]{5,0,4,3,2,1:T(8,128)(2,1)}, u32[]{:S(2)}, u32[]{:S(2)}) async-start(bf16[32,2,1,1,3,2048]{5,0,4,3,2,1:T(8,128)(2,1)} %copy.62), calls=%async_computation.1 | async-start | bytes 1572864 | tf_op jit(solution)/shard_map/all_to_all | solution.py:27
  97.8 110.6 %all-to-all-start.2 = ((bf16[4,512,2304]{2,1,0:T(8,128)(2,1)}), bf16[4,512,2304]{2,1,0:T(8,128)(2,1)}, u32[]{:S(2)}, u32[]{:S(2)}) async-start(bf16[4,512,2304]{2,1,0:T(8,128)(2,1)} %stack.2), calls=%async_computation.2 | async-start | bytes 18874368 | tf_op jit(solution)/shard_map/all_to_all | solution.py:42
  103.7 3.5 %copy-start.4 = (bf16[32,2,1,1,3,2048]{5,0,4,3,2,1:T(8,128)(2,1)S(1)}, bf16[32,2,1,1,3,2048]{5,0,4,3,2,1:T(8,128)(2,1)}, u32[]{:S(2)}) copy-start(bf16[32,2,1,1,3,2048]{5,0,4,3,2,1:T(8,128)(2,1)} %all_to_all.63) | copy-start | bytes 2359300
  103.7 227.2 %all-gather.2.cloned.1.call-start = ((), (), s32[]{:S(2)}) async-start(), calls=%async_computation.10 | async-start | bytes 4423680 | tf_op jit(solution)/shard_map/all_gather | solution.py:70
  224.2 25.7 %all-to-all-start.7 = ((bf16[32,2,1,1,3,2048]{5,1,4,3,2,0:T(2,128)(2,1)}), bf16[32,2,1,1,3,2048]{5,1,4,3,2,0:T(2,128)(2,1)S(1)}, u32[]{:S(2)}, u32[]{:S(2)}) async-start(bf16[32,2,1,1,3,2048]{5,1,4,3,2,0:T(2,128)(2,1)} %copy.73), calls=%async_computation.7 | async-start | bytes 1572864 | tf_op jit(solution)/shard_map/all_to_all | solution.py:27
  249.9 27.2 %all-to-all-start.9 = ((bf16[1,128,3,2048]{1,2,0,3:T(4,128)(2,1)}), bf16[1,128,3,2048]{1,2,0,3:T(4,128)(2,1)S(1)}, u32[]{:S(2)}, u32[]{:S(2)}) async-start(bf16[1,128,3,2048]{1,2,0,3:T(4,128)(2,1)} %copy.78), calls=%async_computation.9 | async-start | bytes 4194304 | tf_op jit(solution)/shard_map/all_to_all | solution.py:61
  286.8 30.7 %all-to-all-start.3 = ((bf16[32,2,1,1,3,2048]{5,1,4,3,2,0:T(2,128)(2,1)}), bf16[32,2,1,1,3,2048]{5,1,4,3,2,0:T(2,128)(2,1)}, u32[]{:S(2)}, u32[]{:S(2)}) async-start(bf16[32,2,1,1,3,2048]{5,1,4,3,2,0:T(2,128)(2,1)} %copy.67), calls=%async_computation.3 | async-start | bytes 1572864 | tf_op jit(solution)/shard_map/all_to_all | solution.py:27
  327.9 3.0 copy-start.7
  333.9 1.4 copy-start.6
  334.0 4.3 %copy-start.1 = (bf16[128,2048]{1,0:T(8,128)(2,1)S(1)}, bf16[128,2048]{1,0:T(8,128)(2,1)}, u32[]{:S(2)}) copy-start(bf16[128,2048]{1,0:T(8,128)(2,1)} %param.11) | copy-start | bytes 1572868
Sparse Core Ops, SparseCore 0:
  216.9 40.3 all-gather.1
